TPU v7x, 128 devices: a whole 4x4x4 slice. The times are simulated.
128 devices in a mesh: seg: 4 (over y), expert: 32 (over x, z, core).
Axes of the slice: x: 4, y: 4, z: 4, core: 2. Of those that a mesh axis runs over, the one named last changes fastest.
Arguments:
- frames: bfloat16 [32768, 1536], P(('seg', 'expert')), may hold values from -6 to 6
- expert_ids: int32 [32768, 2], P(('seg', 'expert')), may hold values from 0 to 31, all different within a row; in each aligned block of 256 rows (0 to 255, 256 to 511, ...) at most 24 rows name the same one
- gate_weights: float32 [32768, 2], P(('seg', 'expert')), may hold values from 0.2 to 1
- up_weight: bfloat16 [32, 1536, 2048], P('expert'), may hold values from -0.15625 to 0.15625
- down_weight: bfloat16 [32, 2048, 1536], P('expert'), may hold values from -0.125 to 0.125
- out_weight: bfloat16 [1536, 64], replicated, may hold values from -0.15625 to 0.15625
- in_conv: bfloat16 [7, 64, 2048], replicated, may hold values from -0.25 to 0.25
- snake_first: float32 [2048], replicated, may hold values from 0.5 to 2
- first_up: bfloat16 [16, 2048, 512], P(None, None, 'seg'), may hold values from -0.09375 to 0.09375
Outputs:
- features: float32 [4, 65536, 512], P(None, 'expert', 'seg')
Inputs may be any that keep to these rules, and one draw needn't show every extreme that they name: `expert_ids`: in each aligned block of 256 rows (the rows of one device) no expert is named by more than 24 of the block's choices, and some block reaches 24; the two ids of a token differ.
All inputs are finite; a program needn't handle non-finite values.
Results may differ from a plain program's by a relative error of at most 0.005.
Values may be sent and summed in bfloat16 or wider, within the bound.
A program may use at most 128 MiB of HBM per device.

v0:
```python
import jax
import jax.numpy as jnp
from jax import lax
from jax.sharding import PartitionSpec as P


def with_halo(value, sides, width):
    for axis, dim in sides:
        size, length = (lax.axis_size(axis), value.shape[dim])
        up = [(i, (i + 1) % size) for i in range(size - 1)]
        down = [(j, i) for i, j in up]
        last = lax.slice_in_dim(value, length - width, length, axis=dim)
        leading = lax.slice_in_dim(value, 0, width, axis=dim)
        before = lax.ppermute(last, axis, up)
        after = lax.ppermute(leading, axis, down)
        value = jnp.concatenate([before, value, after], axis=dim)
    return value


def snake_act(values, alpha_row):
    return values + jnp.sin(alpha_row * values) ** 2 / alpha_row


def slot_dest(expert_ids, num_experts, capacity):
    flat_ids = expert_ids.reshape(-1)
    one_hot = (flat_ids[:, None] == jnp.arange(num_experts, dtype=jnp.int32)[None, :]).astype(
        jnp.int32
    )
    before = jnp.cumsum(one_hot, axis=0) - one_hot
    return flat_ids * capacity + jnp.sum(before * one_hot, axis=1)


def conv_seven(padded, weights, length):
    windows = [
        lax.slice_in_dim(padded, tap_index, tap_index + length, axis=1) for tap_index in range(7)
    ]
    stacked = jnp.concatenate(windows, axis=2)
    return jnp.einsum(
        "klc,co->klo",
        stacked,
        weights.reshape(-1, weights.shape[2]),
        preferred_element_type=jnp.float32,
    )


def upsample(padded, weights, length):
    prev_rows = padded[:, 0:length]
    here_rows = padded[:, 1 : length + 1]
    next_rows = padded[:, 2 : length + 2]
    middle = jnp.einsum(
        "klc,rco->klro", here_rows, weights[4:12], preferred_element_type=jnp.float32
    )
    early_part = jnp.einsum(
        "klc,rco->klro", prev_rows, weights[12:16], preferred_element_type=jnp.float32
    )
    later_part = jnp.einsum(
        "klc,rco->klro", next_rows, weights[0:4], preferred_element_type=jnp.float32
    )
    joined = middle + jnp.concatenate([early_part, later_part], axis=2)
    return joined.reshape(padded.shape[0], length * 8, weights.shape[2])


def local(
    frames,
    expert_ids,
    gate_weights,
    up_weight,
    down_weight,
    out_weight,
    in_conv,
    snake_first,
    first_up,
):
    tok_rows, model_dim = frames.shape
    num_experts = lax.axis_size("expert")
    capacity = 3 * tok_rows // num_experts
    dest_slot = slot_dest(expert_ids, num_experts, capacity)
    source_rows = jnp.repeat(frames, 2, axis=0)
    send_buffer = (
        jnp.zeros((num_experts * capacity, model_dim), jnp.bfloat16).at[dest_slot].set(source_rows)
    )
    send_buffer = send_buffer.reshape(num_experts, capacity, model_dim)
    upper_weight = up_weight[0]
    lower_weight = down_weight[0]
    received = lax.all_to_all(send_buffer, "expert", split_axis=0, concat_axis=0, tiled=True)
    count_src, count_rows, _ = received.shape
    flat_rows = received.reshape(count_src * count_rows, model_dim)
    hidden_units = jax.nn.gelu(
        jnp.dot(flat_rows, upper_weight, preferred_element_type=jnp.float32), approximate=True
    ).astype(jnp.bfloat16)
    expert_out = jnp.dot(hidden_units, lower_weight, preferred_element_type=jnp.float32).astype(
        jnp.bfloat16
    )
    processed = expert_out.reshape(count_src, count_rows, expert_out.shape[1])
    returned = lax.all_to_all(processed, "expert", split_axis=0, concat_axis=0, tiled=True)
    picked_rows = returned.reshape(num_experts * capacity, model_dim)[dest_slot]
    picked = jnp.dot(picked_rows, out_weight, preferred_element_type=jnp.float32)
    lat_dim = out_weight.shape[1]
    gated = jnp.sum(picked.reshape(tok_rows, 2, lat_dim) * gate_weights[:, :, None], axis=1)
    latent = jnp.dot(frames, out_weight, preferred_element_type=jnp.float32) + gated
    latent_low = latent.astype(jnp.bfloat16)
    lat_padded = with_halo(latent_low, (("expert", 0),), 3)
    first_in = conv_seven(lat_padded[None], in_conv, tok_rows)[0]
    act_first = snake_act(first_in, snake_first).astype(jnp.bfloat16)
    pad_first = with_halo(act_first, (("expert", 0),), 1)
    return upsample(lax.all_gather(pad_first[None], "seg", axis=0, tiled=True), first_up, tok_rows)


def solution(mesh):
    placed = (
        P(("seg", "expert"), None),
        P(("seg", "expert"), None),
        P(("seg", "expert"), None),
        P("expert", None, None),
        P("expert", None, None),
        P(),
        P(),
        P(),
        P(None, None, "seg"),
    )
    return jax.shard_map(
        local, mesh=mesh, in_specs=placed, out_specs=P(None, "expert", "seg"), check_vma=False
    )
```

profile of v0, /device:TPU:1, one launch (start us, length us, event | category | flops | bytes accessed | tf_op | source)
XLA Modules:
  0.0 225.3 jit_solution(10748287871956991975)
XLA Ops:
  8.8 1.2 reduce-window.6
  10.2 2.0 broadcast_in_dim.9
  12.2 1.5 reshape.99
  13.8 5.5 %scatter_custom_fusion = bf16[768,1536]{1,0:T(8,128)(2,1)} fusion(s32[512]{0:T(512)S(1)} %bitcast.91, bf16[512,1536]{1,0:T(8,128)(2,1)} %reshape.99, bf16[]{:T(256)} %constant.9.clone.1), kind=kCustom, calls=%fused_computation.35 | custom fusion | bytes 2359808 | tf_op jit(solution)/shard_map/scatter | solution.py:80
  19.3 41.0 %all_to_all.10 = bf16[32,24,1536]{2,1,0:T(8,128)(2,1)} all-to-all(bf16[32,24,1536]{2,1,0:T(8,128)(2,1)} %bitcast.87), channel_id=1, replica_groups=mesh['seg'=4,'expert'=32] {'expert'}, dimensions={0} | all-to-all | bytes 4718592 | tf_op jit(solution)/shard_map/all_to_all | solution.py:85
  60.3 16.6 %fusion.17 = bf16[768,1536]{1,0:T(8,128)(2,1)} fusion(bf16[1,2048,1536]{2,1,0:T(8,128)(2,1)} %param.13, bf16[768,1536]{1,0:T(8,128)(2,1)} %bitcast.89, bf16[1,1536,2048]{2,1,0:T(8,128)(2,1)} %param.12), kind=kOutput, calls=%fused_computation.25 | convolution fusion | flops 9679011840 | bytes 17301504 | tf_op jit(solution)/shard_map/dot_general | solution.py:91
  76.9 4.7 %all-to-all-start.1 = ((bf16[32,24,1536]{2,1,0:T(8,128)(2,1)}), bf16[32,24,1536]{2,1,0:T(8,128)(2,1)}, u32[]{:S(2)}, u32[]{:S(2)}) async-start(bf16[32,24,1536]{2,1,0:T(8,128)(2,1)} %bitcast.88), calls=%async_computation.1 | async-start | bytes 4718592 | tf_op jit(solution)/shard_map/all_to_all | solution.py:95
  81.9 31.1 %all-to-all-done.1 = bf16[32,24,1536]{2,1,0:T(8,128)(2,1)} async-done(((bf16[32,24,1536]{2,1,0:T(8,128)(2,1)}), bf16[32,24,1536]{2,1,0:T(8,128)(2,1)}, u32[]{:S(2)}, u32[]{:S(2)}) %all-to-all-start.1) | async-done | bytes 2359328 | tf_op jit(solution)/shard_map/all_to_all | solution.py:95
  112.9 5.6 %gather_fusion = bf16[512,1536]{1,0:T(8,128)(2,1)S(1)} fusion(bf16[768,1536]{1,0:T(8,128)(2,1)} %bitcast.8, s32[1024]{0:T(1024)S(1)} %pad_clamp_fusion), kind=kCustom, calls=%fused_computation | custom fusion | bytes 3147776 | tf_op jit(solution)/shard_map/gather | solution.py:96
  118.5 1.5 fusion.52
  120.5 1.5 fusion.37
  122.1 2.4 %collective-permute-start = (bf16[3,64]{0,1:T(8,128)(2,1)S(1)}, bf16[3,64]{0,1:T(8,128)(2,1)S(1)}, u32[]{:S(2)}, u32[]{:S(2)}) collective-permute-start(bf16[3,64]{0,1:T(8,128)(2,1)S(1)} %get-tuple-element.7), channel_id=1, source_target_pairs={{0,1},{1,2},{2,3},{3,4},{4,5},{5,6},{6,7},{7,8},{8,9},{9,10},{10,1... | collective-permute-start | bytes 1160 | tf_op jit(solution)/shard_map/ppermute | solution.py:14
  124.5 2.2 collective-permute-start.1
  126.7 2.9 %collective-permute-done.1 = bf16[3,64]{0,1:T(8,128)(2,1)S(1)} collective-permute-done((bf16[3,64]{0,1:T(8,128)(2,1)S(1)}, bf16[3,64]{0,1:T(8,128)(2,1)S(1)}, u32[]{:S(2)}, u32[]{:S(2)}) %collective-permute-start.1) | collective-permute-done | bytes 416 | tf_op jit(solution)/shard_map/ppermute | solution.py:15
  130.2 8.7 %add_convert_fusion = bf16[256,2048]{1,0:T(8,128)(2,1)S(1)} fusion(f32[2048]{0:T(1024)S(1)} %copy-done.3, bf16[448,2048]{1,0:T(8,128)(2,1)S(1)} %bitcast.86, bf16[1,256,448]{1,2,0:T(8,128)(2,1)S(1)} %slice_dynamic-update-slice_fusion), kind=kOutput, calls=%fused_computation.34 | convolution fusion | flops 472383488 | bytes 3121152 | tf_op jit(solution)/shard_map/klc,co->klo/dot_general | solution.py:38
  138.9 1.9 collective-permute-start.2
  140.9 2.4 %collective-permute-start.3 = (bf16[1,2048]{1,0:T(2,128)(2,1)S(1)}, bf16[1,2048]{1,0:T(2,128)(2,1)S(1)}, u32[]{:S(2)}, u32[]{:S(2)}) collective-permute-start(bf16[1,2048]{1,0:T(2,128)(2,1)S(1)} %get-tuple-element.6), channel_id=1, source_target_pairs={{1,0},{2,1},{3,2},{4,3},{5,4},{6,5},{7,6},{8,7},{9,8},{10,9},{11,1... | collective-permute-start | bytes 12296 | tf_op jit(solution)/shard_map/ppermute | solution.py:15
  143.3 2.6 %collective-permute-done.3 = bf16[1,2048]{1,0:T(2,128)(2,1)S(1)} collective-permute-done((bf16[1,2048]{1,0:T(2,128)(2,1)S(1)}, bf16[1,2048]{1,0:T(2,128)(2,1)S(1)}, u32[]{:S(2)}, u32[]{:S(2)}) %collective-permute-start.3) | collective-permute-done | bytes 4128 | tf_op jit(solution)/shard_map/ppermute | solution.py:15
  145.8 1.3 maximum_bitcast_fusion
  147.2 52.8 %all-gather.4.cloned.1.call-done = bf16[4,258,2048]{2,1,0:T(8,128)(2,1)} async-done(((bf16[1,258,2048]{2,1,0:T(8,128)(2,1)}), bf16[4,258,2048]{2,1,0:T(8,128)(2,1)}) %all-gather.4.cloned.1.call-update) | async-done | bytes 4227088 | tf_op jit(solution)/shard_map/all_gather | solution.py:106
  200.0 5.3 %fusion.13 = f32[4,256,4,128]{3,1,2,0:T(8,128)S(1)} fusion(bf16[4,258,2048]{2,1,0:T(8,128)(2,1)} %all-gather.4.cloned.1.call-done, bf16[16,2048,128]{2,1,0:T(8,128)(2,1)} %param.17), kind=kOutput, calls=%fused_computation.18 | convolution fusion | flops 2147483648 | bytes 8388608 | tf_op jit(solution)/shard_map/klc,rco->klro/dot_general | solution.py:53
  205.3 4.1 %fusion.12 = f32[4,256,4,128]{3,1,2,0:T(8,128)S(1)} fusion(bf16[4,258,2048]{2,1,0:T(8,128)(2,1)S(1)} %copy-done.2, bf16[16,2048,128]{2,1,0:T(8,128)(2,1)} %param.17), kind=kOutput, calls=%fused_computation.16 | convolution fusion | flops 2147483648 | bytes 8388608 | tf_op jit(solution)/shard_map/klc,rco->klro/dot_general | solution.py:56
  209.5 4.5 %maximum_add_fusion = f32[4,256,8,128]{3,1,2,0:T(8,128)S(1)} fusion(f32[4,256,4,128]{3,1,2,0:T(8,128)S(1)} %fusion.12, f32[4,256,4,128]{3,1,2,0:T(8,128)S(1)} %fusion.13, bf16[16,2048,128]{2,1,0:T(8,128)(2,1)S(1)} %bitcast.95, bf16[4,258,2048]{2,1,0:T(8,128)(2,1)S(1)} %copy-done.2), kind=kOutput, calls=%fused_computation.21 | convolution fusion | flops 4297064448 | bytes 16777216 | tf_op jit(solution)/shard_map/klc,rco->klro/dot_general | solution.py:50
  214.0 4.4 %copy.33 = f32[4,256,8,128]{3,2,1,0:T(8,128)} copy(f32[4,256,8,128]{3,1,2,0:T(8,128)S(1)} %maximum_add_fusion) | data formatting | bytes 8388608 | tf_op jit(solution)/shard_map/add | solution.py:59
  (43 shorter events, 4.0 us)
Async XLA Ops:
  6.5 123.6 %copy-start = (bf16[7,64,2048]{2,1,0:T(8,128)(2,1)S(1)}, bf16[7,64,2048]{2,1,0:T(8,128)(2,1)}, u32[]{:S(2)}) copy-start(bf16[7,64,2048]{2,1,0:T(8,128)(2,1)} %param.15) | copy-start | bytes 5505028
  76.9 4.8 %copy-start.1 = (f32[256,2]{0,1:T(2,128)S(1)}, f32[256,2]{0,1:T(2,128)}, u32[]{:S(2)}) copy-start(f32[256,2]{0,1:T(2,128)} %param.11) | copy-start | bytes 6148
  76.9 36.0 %all-to-all-start.1 = ((bf16[32,24,1536]{2,1,0:T(8,128)(2,1)}), bf16[32,24,1536]{2,1,0:T(8,128)(2,1)}, u32[]{:S(2)}, u32[]{:S(2)}) async-start(bf16[32,24,1536]{2,1,0:T(8,128)(2,1)} %bitcast.88), calls=%async_computation.1 | async-start | bytes 4718592 | tf_op jit(solution)/shard_map/all_to_all | solution.py:95
  81.6 118.3 %all-gather.4.cloned.1.call-start = ((), (), s32[]{:S(2)}) async-start(), calls=%async_computation.2 | async-start | bytes 5406720 | tf_op jit(solution)/shard_map/all_gather | solution.py:106
  118.5 11.6 %copy-start.3 = (f32[2048]{0:T(1024)S(1)}, f32[2048]{0:T(1024)}, u32[]{:S(2)}) copy-start(f32[2048]{0:T(1024)} %param.16) | copy-start | bytes 24580
  122.1 4.6 %collective-permute-start = (bf16[3,64]{0,1:T(8,128)(2,1)S(1)}, bf16[3,64]{0,1:T(8,128)(2,1)S(1)}, u32[]{:S(2)}, u32[]{:S(2)}) collective-permute-start(bf16[3,64]{0,1:T(8,128)(2,1)S(1)} %get-tuple-element.7), channel_id=1, source_target_pairs={{0,1},{1,2},{2,3},{3,4},{4,5},{5,6},{6,7},{7,8},{8,9},{9,10},{10,1... | collective-permute-start | bytes 1160 | tf_op jit(solution)/shard_map/ppermute | solution.py:14
  124.5 5.1 %collective-permute-start.1 = (bf16[3,64]{0,1:T(8,128)(2,1)S(1)}, bf16[3,64]{0,1:T(8,128)(2,1)S(1)}, u32[]{:S(2)}, u32[]{:S(2)}) collective-permute-start(bf16[3,64]{0,1:T(8,128)(2,1)S(1)} %get-tuple-element.8), channel_id=1, source_target_pairs={{1,0},{2,1},{3,2},{4,3},{5,4},{6,5},{7,6},{8,7},{9,8},{10,9},{11,1... | collective-permute-start | bytes 1160 | tf_op jit(solution)/shard_map/ppermute | solution.py:15
  138.9 4.3 %collective-permute-start.2 = (bf16[1,2048]{1,0:T(2,128)(2,1)S(1)}, bf16[1,2048]{1,0:T(2,128)(2,1)S(1)}, u32[]{:S(2)}, u32[]{:S(2)}) collective-permute-start(bf16[1,2048]{1,0:T(2,128)(2,1)S(1)} %get-tuple-element.5), channel_id=1, source_target_pairs={{0,1},{1,2},{2,3},{3,4},{4,5},{5,6},{6,7},{7,8},{8,9},{9,10},{10,1... | collective-permute-start | bytes 12296 | tf_op jit(solution)/shard_map/ppermute | solution.py:14
  140.9 5.0 %collective-permute-start.3 = (bf16[1,2048]{1,0:T(2,128)(2,1)S(1)}, bf16[1,2048]{1,0:T(2,128)(2,1)S(1)}, u32[]{:S(2)}, u32[]{:S(2)}) collective-permute-start(bf16[1,2048]{1,0:T(2,128)(2,1)S(1)} %get-tuple-element.6), channel_id=1, source_target_pairs={{1,0},{2,1},{3,2},{4,3},{5,4},{6,5},{7,6},{8,7},{9,8},{10,9},{11,1... | collective-permute-start | bytes 12296 | tf_op jit(solution)/shard_map/ppermute | solution.py:15
  200.0 5.3 %copy-start.2 = (bf16[4,258,2048]{2,1,0:T(8,128)(2,1)S(1)}, bf16[4,258,2048]{2,1,0:T(8,128)(2,1)}, u32[]{:S(2)}) copy-start(bf16[4,258,2048]{2,1,0:T(8,128)(2,1)} %all-gather.4.cloned.1.call-done) | copy-start | bytes 12681220
  200.0 9.4 %slice-start = ((s8[8388608]{0:T(1024)(128)(4,1)}), s8[4194304]{0:T(1024)(128)(4,1)S(1)}, s32[]{:S(2)}) async-start(s8[8388608]{0:T(1024)(128)(4,1)} %bitcast.94), calls=%async_computation.3 | async-start | bytes 8388608
  205.3 4.1 %slice-start.1 = ((s8[8388608]{0:T(1024)(128)(4,1)}), s8[4194304]{0:T(1024)(128)(4,1)S(1)}, s32[]{:S(2)}) async-start(s8[8388608]{0:T(1024)(128)(4,1)} %bitcast.94), calls=%async_computation.4 | async-start | bytes 8388608
Sparse Core Ops, SparseCore 0:
  147.3 52.6 all-gather.3
where the time goes:
time: 226 us; the launch traced here: 225 us
  waiting for transfers between devices  89.4 us (40%)
  matrix products  42.3 us (19%)
  blocking collectives  41 us (18%)
  local copies, waits for them, and re-layouts  21.4 us (9%)
  between operations  13.7 us (6%)
  starting transfers between devices  13.6 us (6%)
  other arithmetic  3.95 us (2%)
    all_gather x1, waiting for transfers between devices, local(): lax.all_gather(pad_first[None], 'seg', axis=0, tiled=True)  52.8 us
    all_to_all x1, blocking collectives, local(): lax.all_to_all(send_buffer, 'expert', split_axis=0, concat_axis=0, tiled=...  41 us
    all_to_all x1, waiting for transfers between devices, local(): lax.all_to_all(processed, 'expert', split_axis=0, concat_axis=0, tiled=True)  31.1 us
    dot_general x1, matrix products, local(): jnp.dot(hidden_units, lower_weight, preferred_element_type=jnp.float32)  16.6 us
    dot_general x1, matrix products, conv_seven(): jnp.einsum('klc,co->klo', stacked, weights.reshape(-1, weights.shape[2]),...  8.72 us
    gather x1, local copies, waits for them, and re-layouts, local(): picked_rows = returned.reshape(num_experts * capacity, model_dim)[dest_slot]  5.57 us
    scatter x1, local copies, waits for them, and re-layouts, local(): jnp.zeros((num_experts * capacity, model_dim), jnp.bfloat16).at[dest_slot]  5.52 us
    ppermute x2, waiting for transfers between devices, with_halo(): after = lax.ppermute(leading, axis, down)  5.43 us
  transfers between devices with their start and end apart: 6, of which 4 were waited for; matrix products, arithmetic and copies ran while one was open for 0% of the time, Pallas kernels for 0%

commit v1 on v0

--- a/solution.py
+++ b/solution.py
@@ -2,6 +2,11 @@
 import jax.numpy as jnp
 from jax import lax
 from jax.sharding import PartitionSpec as P
+
+
+def swapped_in(x, axis, dim):
+    sent = jnp.stack([x] * lax.axis_size(axis))
+    return jnp.concatenate(lax.all_to_all(sent, axis, 0, 0), axis=dim)
 
 
 def with_halo(value, sides, width):
@@ -103,7 +108,7 @@
     first_in = conv_seven(lat_padded[None], in_conv, tok_rows)[0]
     act_first = snake_act(first_in, snake_first).astype(jnp.bfloat16)
     pad_first = with_halo(act_first, (("expert", 0),), 1)
-    return upsample(lax.all_gather(pad_first[None], "seg", axis=0, tiled=True), first_up, tok_rows)
+    return upsample(swapped_in(pad_first[None], "seg", 0), first_up, tok_rows)
 
 
 def solution(mesh):

time: 226 us -> 208 us (0.920)
  blocking collectives: 41 us -> 95 us
  waiting for transfers between devices: 89.4 us -> 36.5 us
  between operations: 13.7 us -> 0.25 us
  matrix products: 42.3 us -> 37.6 us
    all_to_all x0 -> x1, blocking collectives: none -> 54 us  [swapped_in(): return jnp.concatenate(lax.all_to_all(sent, axis, 0, 0), axis=dim)]
    all_gather x1 -> x0, waiting for transfers between devices: 52.8 us -> none  [local(): lax.all_gather(pad_first[None], 'seg', axis=0, tiled=True)]
    dot_general x1, matrix products: 5.32 us -> 2.32 us  [upsample(): jnp.einsum('klc,rco->klro', prev_rows, weights[12:16], preferred_element_...]
  transfers between devices with their start and end apart: 6 -> 5, of which waited for: 4 -> 3; matrix products, arithmetic and copies ran while one was open for 0% -> 0% of each run, Pallas kernels for 0% -> 0%
where the time goes in v1:
time: 208 us
  blocking collectives  95 us (46%)
  matrix products  37.6 us (18%)
  waiting for transfers between devices  36.5 us (18%)
  local copies, waits for them, and re-layouts  22 us (11%)
  starting transfers between devices  13.6 us (7%)
  other arithmetic  2.92 us (1%)
    all_to_all x1, blocking collectives, swapped_in(): return jnp.concatenate(lax.all_to_all(sent, axis, 0, 0), axis=dim)  54 us
    all_to_all x1, blocking collectives, local(): lax.all_to_all(send_buffer, 'expert', split_axis=0, concat_axis=0, tiled=...  41 us
    all_to_all x1, waiting for transfers between devices, local(): lax.all_to_all(processed, 'expert', split_axis=0, concat_axis=0, tiled=True)  31.1 us
    dot_general x1, matrix products, local(): jnp.dot(hidden_units, lower_weight, preferred_element_type=jnp.float32)  16.6 us
    dot_general x1, matrix products, conv_seven(): jnp.einsum('klc,co->klo', stacked, weights.reshape(-1, weights.shape[2]),...  8.72 us
    gather x1, local copies, waits for them, and re-layouts, local(): picked_rows = returned.reshape(num_experts * capacity, model_dim)[dest_slot]  5.57 us
    scatter x1, local copies, waits for them, and re-layouts, local(): jnp.zeros((num_experts * capacity, model_dim), jnp.bfloat16).at[dest_slot]  5.52 us
    ppermute x2, waiting for transfers between devices, with_halo(): after = lax.ppermute(leading, axis, down)  5.41 us
  transfers between devices with their start and end apart: 5, of which 3 were waited for; matrix products, arithmetic and copies ran while one was open for 0% of the time, Pallas kernels for 0%

profile of v1, /device:TPU:1, one launch (start us, length us, event | category | flops | bytes accessed | tf_op | source)
XLA Modules:
  0.0 207.8 jit_solution(7015443123860901873)
XLA Ops:
  0.0 0.8 broadcast_multiply_fusion
  2.2 1.2 reduce-window.6
  3.7 2.0 broadcast_in_dim.7
  5.6 1.5 reshape.105
  7.3 5.5 %scatter_custom_fusion = bf16[768,1536]{1,0:T(8,128)(2,1)} fusion(s32[512]{0:T(512)S(1)} %bitcast.93, bf16[512,1536]{1,0:T(8,128)(2,1)} %reshape.105, bf16[]{:T(256)} %constant.9.clone.1), kind=kCustom, calls=%fused_computation.35 | custom fusion | bytes 2359808 | tf_op jit(solution)/shard_map/scatter | solution.py:85
  12.8 41.0 %all_to_all.15 = bf16[32,24,1536]{2,1,0:T(8,128)(2,1)} all-to-all(bf16[32,24,1536]{2,1,0:T(8,128)(2,1)} %bitcast.86), channel_id=1, replica_groups=mesh['seg'=4,'expert'=32] {'expert'}, dimensions={0} | all-to-all | bytes 4718592 | tf_op jit(solution)/shard_map/all_to_all | solution.py:90
  53.7 16.6 %fusion.17 = bf16[768,1536]{1,0:T(8,128)(2,1)} fusion(bf16[1,2048,1536]{2,1,0:T(8,128)(2,1)} %param.13, bf16[768,1536]{1,0:T(8,128)(2,1)} %bitcast.91, bf16[1,1536,2048]{2,1,0:T(8,128)(2,1)} %param.12), kind=kOutput, calls=%fused_computation.25 | convolution fusion | flops 9679011840 | bytes 17301504 | tf_op jit(solution)/shard_map/dot_general | solution.py:96
  70.4 4.7 %all-to-all-start.1 = ((bf16[32,24,1536]{2,1,0:T(8,128)(2,1)}), bf16[32,24,1536]{2,1,0:T(8,128)(2,1)}, u32[]{:S(2)}, u32[]{:S(2)}) async-start(bf16[32,24,1536]{2,1,0:T(8,128)(2,1)} %bitcast.90), calls=%async_computation.1 | async-start | bytes 4718592 | tf_op jit(solution)/shard_map/all_to_all | solution.py:100
  75.3 31.1 %all-to-all-done.1 = bf16[32,24,1536]{2,1,0:T(8,128)(2,1)} async-done(((bf16[32,24,1536]{2,1,0:T(8,128)(2,1)}), bf16[32,24,1536]{2,1,0:T(8,128)(2,1)}, u32[]{:S(2)}, u32[]{:S(2)}) %all-to-all-start.1) | async-done | bytes 2359328 | tf_op jit(solution)/shard_map/all_to_all | solution.py:100
  106.4 5.6 %gather_fusion = bf16[512,1536]{1,0:T(8,128)(2,1)S(1)} fusion(bf16[768,1536]{1,0:T(8,128)(2,1)} %bitcast.8, s32[1024]{0:T(1024)S(1)} %pad_clamp_fusion), kind=kCustom, calls=%fused_computation | custom fusion | bytes 3147776 | tf_op jit(solution)/shard_map/gather | solution.py:101
  112.0 1.5 fusion.52
  114.0 1.5 fusion.37
  115.6 2.3 %collective-permute-start = (bf16[3,64]{0,1:T(8,128)(2,1)S(1)}, bf16[3,64]{0,1:T(8,128)(2,1)S(1)}, u32[]{:S(2)}, u32[]{:S(2)}) collective-permute-start(bf16[3,64]{0,1:T(8,128)(2,1)S(1)} %get-tuple-element.7), channel_id=1, source_target_pairs={{0,1},{1,2},{2,3},{3,4},{4,5},{5,6},{6,7},{7,8},{8,9},{9,10},{10,1... | collective-permute-start | bytes 1160 | tf_op jit(solution)/shard_map/ppermute | solution.py:19
  118.0 2.2 %collective-permute-start.1 = (bf16[3,64]{0,1:T(8,128)(2,1)S(1)}, bf16[3,64]{0,1:T(8,128)(2,1)S(1)}, u32[]{:S(2)}, u32[]{:S(2)}) collective-permute-start(bf16[3,64]{0,1:T(8,128)(2,1)S(1)} %get-tuple-element.8), channel_id=1, source_target_pairs={{1,0},{2,1},{3,2},{4,3},{5,4},{6,5},{7,6},{8,7},{9,8},{10,9},{11,1... | collective-permute-start | bytes 1160 | tf_op jit(solution)/shard_map/ppermute | solution.py:20
  120.2 2.8 %collective-permute-done.1 = bf16[3,64]{0,1:T(8,128)(2,1)S(1)} collective-permute-done((bf16[3,64]{0,1:T(8,128)(2,1)S(1)}, bf16[3,64]{0,1:T(8,128)(2,1)S(1)}, u32[]{:S(2)}, u32[]{:S(2)}) %collective-permute-start.1) | collective-permute-done | bytes 416 | tf_op jit(solution)/shard_map/ppermute | solution.py:20
  123.6 8.7 %add_convert_fusion = bf16[256,2048]{1,0:T(8,128)(2,1)S(1)} fusion(f32[2048]{0:T(1024)S(1)} %copy-done.2, bf16[448,2048]{1,0:T(8,128)(2,1)S(1)} %bitcast.85, bf16[1,256,448]{1,2,0:T(8,128)(2,1)S(1)} %slice_dynamic-update-slice_fusion), kind=kOutput, calls=%fused_computation.34 | convolution fusion | flops 472383488 | bytes 3121152 | tf_op jit(solution)/shard_map/klc,co->klo/dot_general | solution.py:43
  132.4 1.9 collective-permute-start.2
  134.3 2.4 %collective-permute-start.3 = (bf16[1,2048]{1,0:T(2,128)(2,1)S(1)}, bf16[1,2048]{1,0:T(2,128)(2,1)S(1)}, u32[]{:S(2)}, u32[]{:S(2)}) collective-permute-start(bf16[1,2048]{1,0:T(2,128)(2,1)S(1)} %get-tuple-element.6), channel_id=1, source_target_pairs={{1,0},{2,1},{3,2},{4,3},{5,4},{6,5},{7,6},{8,7},{9,8},{10,9},{11,1... | collective-permute-start | bytes 12296 | tf_op jit(solution)/shard_map/ppermute | solution.py:20
  136.7 2.6 %collective-permute-done.3 = bf16[1,2048]{1,0:T(2,128)(2,1)S(1)} collective-permute-done((bf16[1,2048]{1,0:T(2,128)(2,1)S(1)}, bf16[1,2048]{1,0:T(2,128)(2,1)S(1)}, u32[]{:S(2)}, u32[]{:S(2)}) %collective-permute-start.3) | collective-permute-done | bytes 4128 | tf_op jit(solution)/shard_map/ppermute | solution.py:20
  140.1 54.0 %all_to_all.16 = bf16[4,1,258,2048]{3,2,1,0:T(8,128)(2,1)S(1)} all-to-all(bf16[4,1,258,2048]{3,2,1,0:T(8,128)(2,1)S(1)} %stack.3), channel_id=1, replica_groups=mesh['seg'=4,'expert'=32] {'seg'}, dimensions={0} | all-to-all | bytes 8454144 | tf_op jit(solution)/shard_map/all_to_all | solution.py:9
  194.2 2.3 %fusion.12 = f32[4,256,4,128]{3,1,2,0:T(8,128)S(1)} fusion(bf16[4,258,2048]{2,1,0:T(8,128)(2,1)S(1)} %bitcast.87, bf16[16,2048,128]{2,1,0:T(8,128)(2,1)S(1)} %bitcast.97), kind=kOutput, calls=%fused_computation.16 | convolution fusion | flops 2147483648 | bytes 8388608 | tf_op jit(solution)/shard_map/klc,rco->klro/dot_general | solution.py:61
  196.5 2.3 %fusion.13 = f32[4,256,4,128]{3,1,2,0:T(8,128)S(1)} fusion(bf16[4,258,2048]{2,1,0:T(8,128)(2,1)S(1)} %bitcast.88, bf16[16,2048,128]{2,1,0:T(8,128)(2,1)S(1)} %bitcast.97), kind=kOutput, calls=%fused_computation.18 | convolution fusion | flops 2147483648 | bytes 8388608 | tf_op jit(solution)/shard_map/klc,rco->klro/dot_general | solution.py:58
  198.9 4.5 %maximum_add_fusion = f32[4,256,8,128]{3,1,2,0:T(8,128)S(1)} fusion(f32[4,256,4,128]{3,1,2,0:T(8,128)S(1)} %fusion.12, f32[4,256,4,128]{3,1,2,0:T(8,128)S(1)} %fusion.13, bf16[16,2048,128]{2,1,0:T(8,128)(2,1)S(1)} %bitcast.97, bf16[4,258,2048]{2,1,0:T(8,128)(2,1)S(1)} %bitcast.89), kind=kOutput, calls=%fused_computation.21 | convolution fusion | flops 4297064448 | bytes 16777216 | tf_op jit(solution)/shard_map/klc,rco->klro/dot_general | solution.py:55
  203.4 4.4 %copy.33 = f32[4,256,8,128]{3,2,1,0:T(8,128)} copy(f32[4,256,8,128]{3,1,2,0:T(8,128)S(1)} %maximum_add_fusion) | data formatting | bytes 8388608 | tf_op jit(solution)/shard_map/add | solution.py:64
  (40 shorter events, 3.9 us)
Async XLA Ops:
  0.0 123.6 %copy-start = (bf16[7,64,2048]{2,1,0:T(8,128)(2,1)S(1)}, bf16[7,64,2048]{2,1,0:T(8,128)(2,1)}, u32[]{:S(2)}) copy-start(bf16[7,64,2048]{2,1,0:T(8,128)(2,1)} %param.15) | copy-start | bytes 5505028
  70.4 4.7 %copy-start.1 = (f32[256,2]{0,1:T(2,128)S(1)}, f32[256,2]{0,1:T(2,128)}, u32[]{:S(2)}) copy-start(f32[256,2]{0,1:T(2,128)} %param.11) | copy-start | bytes 6148
  70.4 36.0 %all-to-all-start.1 = ((bf16[32,24,1536]{2,1,0:T(8,128)(2,1)}), bf16[32,24,1536]{2,1,0:T(8,128)(2,1)}, u32[]{:S(2)}, u32[]{:S(2)}) async-start(bf16[32,24,1536]{2,1,0:T(8,128)(2,1)} %bitcast.90), calls=%async_computation.1 | async-start | bytes 4718592 | tf_op jit(solution)/shard_map/all_to_all | solution.py:100
  112.0 11.6 %copy-start.2 = (f32[2048]{0:T(1024)S(1)}, f32[2048]{0:T(1024)}, u32[]{:S(2)}) copy-start(f32[2048]{0:T(1024)} %param.16) | copy-start | bytes 24580
  115.6 4.6 %collective-permute-start = (bf16[3,64]{0,1:T(8,128)(2,1)S(1)}, bf16[3,64]{0,1:T(8,128)(2,1)S(1)}, u32[]{:S(2)}, u32[]{:S(2)}) collective-permute-start(bf16[3,64]{0,1:T(8,128)(2,1)S(1)} %get-tuple-element.7), channel_id=1, source_target_pairs={{0,1},{1,2},{2,3},{3,4},{4,5},{5,6},{6,7},{7,8},{8,9},{9,10},{10,1... | collective-permute-start | bytes 1160 | tf_op jit(solution)/shard_map/ppermute | solution.py:19
  118.0 5.1 %collective-permute-start.1 = (bf16[3,64]{0,1:T(8,128)(2,1)S(1)}, bf16[3,64]{0,1:T(8,128)(2,1)S(1)}, u32[]{:S(2)}, u32[]{:S(2)}) collective-permute-start(bf16[3,64]{0,1:T(8,128)(2,1)S(1)} %get-tuple-element.8), channel_id=1, source_target_pairs={{1,0},{2,1},{3,2},{4,3},{5,4},{6,5},{7,6},{8,7},{9,8},{10,9},{11,1... | collective-permute-start | bytes 1160 | tf_op jit(solution)/shard_map/ppermute | solution.py:20
  132.4 4.3 %collective-permute-start.2 = (bf16[1,2048]{1,0:T(2,128)(2,1)S(1)}, bf16[1,2048]{1,0:T(2,128)(2,1)S(1)}, u32[]{:S(2)}, u32[]{:S(2)}) collective-permute-start(bf16[1,2048]{1,0:T(2,128)(2,1)S(1)} %get-tuple-element.5), channel_id=1, source_target_pairs={{0,1},{1,2},{2,3},{3,4},{4,5},{5,6},{6,7},{7,8},{8,9},{9,10},{10,1... | collective-permute-start | bytes 12296 | tf_op jit(solution)/shard_map/ppermute | solution.py:19
  134.3 5.0 %collective-permute-start.3 = (bf16[1,2048]{1,0:T(2,128)(2,1)S(1)}, bf16[1,2048]{1,0:T(2,128)(2,1)S(1)}, u32[]{:S(2)}, u32[]{:S(2)}) collective-permute-start(bf16[1,2048]{1,0:T(2,128)(2,1)S(1)} %get-tuple-element.6), channel_id=1, source_target_pairs={{1,0},{2,1},{3,2},{4,3},{5,4},{6,5},{7,6},{8,7},{9,8},{10,9},{11,1... | collective-permute-start | bytes 12296 | tf_op jit(solution)/shard_map/ppermute | solution.py:20
  139.3 54.9 %slice-start = ((s8[8388608]{0:T(1024)(128)(4,1)}), s8[4194304]{0:T(1024)(128)(4,1)S(1)}, s32[]{:S(2)}) async-start(s8[8388608]{0:T(1024)(128)(4,1)} %bitcast.96), calls=%async_computation.3 | async-start | bytes 8388608
  140.1 54.1 %slice-start.1 = ((s8[8388608]{0:T(1024)(128)(4,1)}), s8[4194304]{0:T(1024)(128)(4,1)S(1)}, s32[]{:S(2)}) async-start(s8[8388608]{0:T(1024)(128)(4,1)} %bitcast.96), calls=%async_computation.4 | async-start | bytes 8388608
